TPU v7x, 128 devices: a whole 4x4x4 slice. The times are simulated.
128 devices in a mesh: req: 4 (over y), tile: 32 (over x, z, core).
Axes of the slice: x: 4, y: 4, z: 4, core: 2. Of those that a mesh axis runs over, the one named last changes fastest.
Arguments:
- image: bfloat16 [8, 4096, 2432], P('req', 'tile'), may hold values from -40 to 40
- text: bfloat16 [8, 154, 2432], P('req'), may hold values from -40 to 40
- pooled: float32 [8, 2432], P('req'), may hold values from -6 to 6
- timesteps: int32 [8], P('req'), may hold values from 0 to 999
- lengths: int32 [8], P('req'), may hold values from 1 to 4096, 16384 in all
- w_time: bfloat16 [256, 2432], replicated, may hold values from -0.375 to 0.375
- w_mod: bfloat16 [2432, 9728], P(None, 'tile'), may hold values from -0.125 to 0.125
- w_img: bfloat16 [2432, 6144], P(None, ('req', 'tile')), may hold values from -0.125 to 0.125
- w_txt: bfloat16 [2432, 6144], P(None, 'tile'), may hold values from -0.125 to 0.125
- q_gain: float32 [64], replicated, may hold values from 1 to 2.5
- k_gain: float32 [64], replicated, may hold values from 1 to 2.5
- text_q_gain: float32 [64], replicated, may hold values from 1 to 2.5
- text_k_gain: float32 [64], replicated, may hold values from 1 to 2.5
Outputs:
- image_attention: bfloat16 [8, 4096, 2048], P('req', 'tile')
- text_attention: bfloat16 [8, 154, 2048], P('req', None, 'tile')
Inputs may be any that keep to these rules, and one draw needn't show every extreme that they name: `lengths`: the image token counts of all 8 requests sum to 16384, and the largest is exactly 4096.
All inputs are finite; a program needn't handle non-finite values. No bound on the sum of `lengths` on one device may be relied on, other than what follows from the above.
Results may differ from a plain program's by a relative error of at most 0.02.
Values may be sent and summed in bfloat16 or wider, within the bound.
A program may use at most 128 MiB of HBM per device.

v0:
```python
import math
import jax
import jax.numpy as jnp
from jax import lax
from jax.sharding import PartitionSpec as P

epsilon = 1e-06


def time_features(step_index, feature_count):
    half_count = feature_count // 2
    frequency = jnp.exp(-math.log(10000.0) * jnp.arange(half_count, dtype=jnp.float32) / half_count)
    angles = step_index.astype(jnp.float32)[:, None] * frequency[None, :]
    return jnp.concatenate([jnp.cos(angles), jnp.sin(angles)], axis=-1).astype(jnp.bfloat16)


def modulate(tokens, shift, scale):
    values = tokens.astype(jnp.float32)
    center = jnp.mean(values, axis=-1, keepdims=True)
    spread = jnp.mean(jnp.square(values - center), axis=-1, keepdims=True)
    normed = (values - center) * lax.rsqrt(spread + epsilon)
    return (normed * (1.0 + scale.astype(jnp.float32)) + shift.astype(jnp.float32)).astype(
        jnp.bfloat16
    )


def rms_gain(vectors, gain):
    factor = lax.rsqrt(jnp.mean(jnp.square(vectors), axis=-1, keepdims=True) + epsilon)
    return (vectors * factor * gain).astype(jnp.bfloat16)


def pack_heads(qkv, head_dim, q_gain, k_gain):
    lead = qkv.shape[:2]
    head_count = qkv.shape[-1] // (3 * head_dim)
    qkv = qkv.reshape(lead + (head_count, 3, head_dim))
    return jnp.concatenate(
        [
            rms_gain(qkv[:, :, :, 0:1, :], q_gain),
            rms_gain(qkv[:, :, :, 1:2, :], k_gain),
            qkv[:, :, :, 2:3, :].astype(jnp.bfloat16),
        ],
        axis=3,
    ).reshape(lead + (head_count, 3 * head_dim))


def local(
    image,
    text,
    pooled,
    timesteps,
    lengths,
    w_time,
    w_mod,
    w_img,
    w_txt,
    q_gain,
    k_gain,
    text_q_gain,
    text_k_gain,
):
    tile_count = lax.axis_size("tile")
    group_count, local_rows, model_width = image.shape
    seq_len = local_rows * tile_count
    text_len = text.shape[1]
    head_dim = q_gain.shape[0]
    heads_here = w_txt.shape[1] // (3 * head_dim)
    score_scale = head_dim ** (-0.5)
    block = min(512, seq_len)
    features = time_features(timesteps, w_time.shape[0])
    cond_act = jax.nn.silu(
        pooled + jnp.dot(features, w_time, preferred_element_type=jnp.float32)
    ).astype(jnp.bfloat16)
    mod_part = jnp.dot(cond_act, w_mod, preferred_element_type=jnp.float32).astype(jnp.bfloat16)
    modulation = lax.all_gather(mod_part, "tile", axis=1, tiled=True)
    h_img = modulate(
        image,
        modulation[:, None, 0:model_width],
        modulation[:, None, model_width : 2 * model_width],
    )
    qkv_img = jnp.einsum(
        "gpd,dc->gpc",
        h_img,
        lax.all_gather(w_img, ("req", "tile"), axis=1, tiled=True),
        preferred_element_type=jnp.float32,
    )
    packed = pack_heads(qkv_img, head_dim, q_gain, k_gain)
    by_head = lax.all_to_all(packed, "tile", split_axis=2, concat_axis=1, tiled=True)
    by_head = by_head.reshape(group_count, seq_len, heads_here, 3, head_dim)
    h_txt = modulate(
        text,
        modulation[:, None, 2 * model_width : 3 * model_width],
        modulation[:, None, 3 * model_width : 4 * model_width],
    )
    qkv_txt = jnp.einsum("gtd,dc->gtc", h_txt, w_txt, preferred_element_type=jnp.float32).reshape(
        group_count, text_len, heads_here, 3, head_dim
    )
    text_queries = jnp.moveaxis(rms_gain(qkv_txt[:, :, :, 0, :], text_q_gain), 2, 1)
    text_keys = jnp.moveaxis(rms_gain(qkv_txt[:, :, :, 1, :], text_k_gain), 2, 1)
    text_values = jnp.moveaxis(qkv_txt[:, :, :, 2, :].astype(jnp.bfloat16), 2, 1)
    image_queries = jnp.moveaxis(by_head[:, :, :, 0, :], 2, 1)
    image_keys = jnp.moveaxis(by_head[:, :, :, 1, :], 2, 1)
    image_values = jnp.moveaxis(by_head[:, :, :, 2, :], 2, 1)
    slot_live = (jnp.arange(seq_len, dtype=jnp.int32)[None, :] < lengths[:, None]).astype(
        jnp.float32
    )
    keys = jnp.concatenate([text_keys, image_keys], axis=2)
    values = jnp.concatenate([text_values, image_values], axis=2)
    key_mask = jnp.concatenate([jnp.ones((group_count, text_len), jnp.float32), slot_live], axis=1)

    def attend_block(query_block):
        scores = (
            jnp.einsum("ghqe,ghke->ghqk", query_block, keys, preferred_element_type=jnp.float32)
            * score_scale
        )
        weights = jnp.exp(scores) * key_mask[:, None, None, :]
        total = jnp.sum(weights, axis=-1)
        summed = jnp.einsum(
            "ghqk,ghke->ghqe",
            weights.astype(jnp.bfloat16),
            values,
            preferred_element_type=jnp.float32,
        )
        return summed / total[..., None]

    text_result = attend_block(text_queries)
    block_count = seq_len // block
    query_blocks = jnp.moveaxis(
        image_queries.reshape(group_count, heads_here, block_count, block, head_dim), 2, 0
    )
    image_result = lax.map(attend_block, query_blocks)
    image_result = jnp.moveaxis(image_result, 0, 2).reshape(
        group_count, heads_here, seq_len, head_dim
    )
    image_result = image_result * slot_live[:, None, :, None]
    image_heads = (
        jnp.moveaxis(image_result, 1, 2)
        .reshape(group_count, seq_len, heads_here * head_dim)
        .astype(jnp.bfloat16)
    )
    image_attention = lax.all_to_all(image_heads, "tile", split_axis=1, concat_axis=2, tiled=True)
    text_attention = (
        jnp.moveaxis(text_result, 1, 2)
        .reshape(group_count, text_len, heads_here * head_dim)
        .astype(jnp.bfloat16)
    )
    return (image_attention, text_attention)


def solution(mesh):
    in_specs = (
        P("req", "tile", None),
        P("req", None, None),
        P("req", None),
        P("req"),
        P("req"),
        P(),
        P(None, "tile"),
        P(None, ("req", "tile")),
        P(None, "tile"),
        P(),
        P(),
        P(),
        P(),
    )
    out_specs = (P("req", "tile", None), P("req", None, "tile"))
    return jax.shard_map(local, mesh=mesh, in_specs=in_specs, out_specs=out_specs, check_vma=False)
```

profile of v0, /device:TPU:1, one launch (start us, length us, event | category | flops | bytes accessed | tf_op | source)
XLA Modules:
  0.0 318.6 jit_solution(9887825131999593207)
XLA Ops:
  10.7 26.9 %all-gather = bf16[32,304,2]{1,2,0:T(2,128)(2,1)S(1)} all-gather(bf16[1,304,2]{1,2,0:T(2,128)(2,1)S(1)} %fusion.59), channel_id=1, replica_groups=mesh['req'=4,'tile'=32] {'tile'}, dimensions={0}, use_global_device_ids=true | all-gather | bytes 40128 | tf_op jit(solution)/shard_map/all_gather | solution.py:74
  42.6 72.7 %all-gather.3.cloned.1.call-done = bf16[2432,6144]{0,1:T(8,128)(2,1)} async-done(((bf16[2432,48]{0,1:T(8,128)(2,1)}), bf16[2432,6144]{0,1:T(8,128)(2,1)}) %all-gather.3.cloned.1.call-update) | async-done | bytes 29884432 | tf_op jit(solution)/shard_map/all_gather | solution.py:83
  115.3 13.6 %fusion.26 = f32[2,128,6144]{1,2,0:T(8,128)S(1)} fusion(bf16[2432,6144]{0,1:T(8,128)(2,1)} %all-gather.3.cloned.1.call-done, bf16[2,128,2432]{2,1,0:T(8,128)(2,1)S(1)} %copy-done.3, f32[2,2432]{1,0:T(2,128)S(1)} %get-tuple-element.69, f32[2,2432]{1,0:T(2,128)S(1)} %get-tuple-element.67, f32[2,128]{1,0:T(2,128)S(1)} %add_rsqrt_fusion.5, ...), kind=kOutput, calls=%fused_computation.14 | convolution fusion | flops 7654146048 | bytes 37462016 | tf_op jit(solution)/shard_map/gpd,dc->gpc/dot_general | solution.py:80
  133.1 6.2 %all-to-all-start = ((bf16[2,128,32,192]{1,3,0,2:T(8,128)(2,1)}), bf16[2,128,32,192]{1,3,0,2:T(8,128)(2,1)}, u32[]{:S(2)}, u32[]{:S(2)}) async-start(bf16[2,128,32,192]{1,3,0,2:T(8,128)(2,1)} %copy.78), calls=%async_computation | async-start | bytes 6291456 | tf_op jit(solution)/shard_map/all_to_all | solution.py:87
  141.5 3.0 fusion.35
  145.4 33.8 %all-to-all-done = bf16[2,128,32,192]{1,3,0,2:T(8,128)(2,1)} async-done(((bf16[2,128,32,192]{1,3,0,2:T(8,128)(2,1)}), bf16[2,128,32,192]{1,3,0,2:T(8,128)(2,1)}, u32[]{:S(2)}, u32[]{:S(2)}) %all-to-all-start) | async-done | bytes 3145760 | tf_op jit(solution)/shard_map/all_to_all | solution.py:87
  179.2 5.6 %copy.79 = bf16[2,32,128,1,192]{2,1,4,0,3:T(8,128)(2,1)} copy(bf16[2,32,128,1,192]{2,4,0,1,3:T(8,128)(2,1)} %bitcast.11) | data formatting | bytes 6291456 | tf_op jit(solution)/shard_map/all_to_all | solution.py:87
  184.8 5.8 %reshape.273 = bf16[2,4096,1,3,64]{1,4,3,0,2:T(8,128)(2,1)} reshape(bf16[2,32,128,1,192]{2,1,4,0,3:T(8,128)(2,1)} %copy.79) | data formatting | bytes 6291456 | tf_op jit(solution)/shard_map/reshape | solution.py:88
  195.3 67.5 %while.10 = (s32[]{:T(128)}, f32[8,2,1,512,64]{3,4,1,2,0:T(8,128)}, bf16[8,2,1,512,64]{3,4,1,2,0:T(8,128)(2,1)}, bf16[2,1,4250,64]{2,3,0,1:T(8,128)(2,1)S(1)}, f...) while((s32[]{:T(128)}, f32[8,2,1,512,64]{3,4,1,2,0:T(8,128)}, ...), condition=%wide.region_9.10_spmd, body=%wide.region_7.0_spmd.sunk | while | flops 1140288512 | bytes 37462508 | solution.py:130
  195.3 4.8 %fusion.93 = (f32[2,512]{1,0:T(2,128)S(1)}, f32[2,512,4250]{1,2,0:T(8,128)S(1)}) fusion(f32[2,4250]{1,0:T(2,128)S(1)} %get-tuple-element.137, bf16[2,1,4250,64]{2,3,0,1:T(8,128)(2,1)S(1)} %get-tuple-element.136, bf16[8,2,1,512,64]{3,4,1,2,0:T(8,128)(2,1)} %get-tuple-element.135, s32[]{:T(128)} %get-tuple-element.126), kind=kOutput, calls=%fused_computation.1.clone.1 | convolution fusion | flops 570110976 | bytes 18665680 | tf_op jit(solution)/shard_map/while/body/eval_jaxpr/ghqe,ghke->ghqk/dot_general | solution.py:112
  200.1 3.6 %fusion.94 = f32[8,2,1,512,64]{3,4,1,2,0:T(8,128)} fusion(f32[8,2,1,512,64]{3,4,1,2,0:T(8,128)} %get-tuple-element.127, s32[]{:T(128)} %get-tuple-element.126, bf16[2,1,4250,64]{2,3,0,1:T(8,128)(2,1)S(1)} %get-tuple-element.138, f32[2,512,4250]{1,2,0:T(8,128)S(1)} %get-tuple-element.117, f32[2,4250]{1,0:T(2,128)S(1)} %get-tuple-element.137, ...), kind=kOutput, calls=%fused_computation.9.clone.1 | convolution fusion | flops 570177536 | bytes 18796752 | tf_op jit(solution)/shard_map/while/body/eval_jaxpr/ghqk,ghke->ghqe/dot_general | solution.py:117
  203.7 4.8 %fusion.93 = (f32[2,512]{1,0:T(2,128)S(1)}, f32[2,512,4250]{1,2,0:T(8,128)S(1)}) fusion(f32[2,4250]{1,0:T(2,128)S(1)} %get-tuple-element.137, bf16[2,1,4250,64]{2,3,0,1:T(8,128)(2,1)S(1)} %get-tuple-element.136, bf16[8,2,1,512,64]{3,4,1,2,0:T(8,128)(2,1)} %get-tuple-element.135, s32[]{:T(128)} %get-tuple-element.126), kind=kOutput, calls=%fused_computation.1.clone.1 | convolution fusion | flops 570110976 | bytes 18665680 | tf_op jit(solution)/shard_map/while/body/eval_jaxpr/ghqe,ghke->ghqk/dot_general | solution.py:112
  208.5 3.6 %fusion.94 = f32[8,2,1,512,64]{3,4,1,2,0:T(8,128)} fusion(f32[8,2,1,512,64]{3,4,1,2,0:T(8,128)} %get-tuple-element.127, s32[]{:T(128)} %get-tuple-element.126, bf16[2,1,4250,64]{2,3,0,1:T(8,128)(2,1)S(1)} %get-tuple-element.138, f32[2,512,4250]{1,2,0:T(8,128)S(1)} %get-tuple-element.117, f32[2,4250]{1,0:T(2,128)S(1)} %get-tuple-element.137, ...), kind=kOutput, calls=%fused_computation.9.clone.1 | convolution fusion | flops 570177536 | bytes 18796752 | tf_op jit(solution)/shard_map/while/body/eval_jaxpr/ghqk,ghke->ghqe/dot_general | solution.py:117
  212.1 4.8 %fusion.93 = (f32[2,512]{1,0:T(2,128)S(1)}, f32[2,512,4250]{1,2,0:T(8,128)S(1)}) fusion(f32[2,4250]{1,0:T(2,128)S(1)} %get-tuple-element.137, bf16[2,1,4250,64]{2,3,0,1:T(8,128)(2,1)S(1)} %get-tuple-element.136, bf16[8,2,1,512,64]{3,4,1,2,0:T(8,128)(2,1)} %get-tuple-element.135, s32[]{:T(128)} %get-tuple-element.126), kind=kOutput, calls=%fused_computation.1.clone.1 | convolution fusion | flops 570110976 | bytes 18665680 | tf_op jit(solution)/shard_map/while/body/eval_jaxpr/ghqe,ghke->ghqk/dot_general | solution.py:112
  216.9 3.6 %fusion.94 = f32[8,2,1,512,64]{3,4,1,2,0:T(8,128)} fusion(f32[8,2,1,512,64]{3,4,1,2,0:T(8,128)} %get-tuple-element.127, s32[]{:T(128)} %get-tuple-element.126, bf16[2,1,4250,64]{2,3,0,1:T(8,128)(2,1)S(1)} %get-tuple-element.138, f32[2,512,4250]{1,2,0:T(8,128)S(1)} %get-tuple-element.117, f32[2,4250]{1,0:T(2,128)S(1)} %get-tuple-element.137, ...), kind=kOutput, calls=%fused_computation.9.clone.1 | convolution fusion | flops 570177536 | bytes 18796752 | tf_op jit(solution)/shard_map/while/body/eval_jaxpr/ghqk,ghke->ghqe/dot_general | solution.py:117
  220.6 4.8 %fusion.93 = (f32[2,512]{1,0:T(2,128)S(1)}, f32[2,512,4250]{1,2,0:T(8,128)S(1)}) fusion(f32[2,4250]{1,0:T(2,128)S(1)} %get-tuple-element.137, bf16[2,1,4250,64]{2,3,0,1:T(8,128)(2,1)S(1)} %get-tuple-element.136, bf16[8,2,1,512,64]{3,4,1,2,0:T(8,128)(2,1)} %get-tuple-element.135, s32[]{:T(128)} %get-tuple-element.126), kind=kOutput, calls=%fused_computation.1.clone.1 | convolution fusion | flops 570110976 | bytes 18665680 | tf_op jit(solution)/shard_map/while/body/eval_jaxpr/ghqe,ghke->ghqk/dot_general | solution.py:112
  225.4 3.6 %fusion.94 = f32[8,2,1,512,64]{3,4,1,2,0:T(8,128)} fusion(f32[8,2,1,512,64]{3,4,1,2,0:T(8,128)} %get-tuple-element.127, s32[]{:T(128)} %get-tuple-element.126, bf16[2,1,4250,64]{2,3,0,1:T(8,128)(2,1)S(1)} %get-tuple-element.138, f32[2,512,4250]{1,2,0:T(8,128)S(1)} %get-tuple-element.117, f32[2,4250]{1,0:T(2,128)S(1)} %get-tuple-element.137, ...), kind=kOutput, calls=%fused_computation.9.clone.1 | convolution fusion | flops 570177536 | bytes 18796752 | tf_op jit(solution)/shard_map/while/body/eval_jaxpr/ghqk,ghke->ghqe/dot_general | solution.py:117
  229.0 4.8 %fusion.93 = (f32[2,512]{1,0:T(2,128)S(1)}, f32[2,512,4250]{1,2,0:T(8,128)S(1)}) fusion(f32[2,4250]{1,0:T(2,128)S(1)} %get-tuple-element.137, bf16[2,1,4250,64]{2,3,0,1:T(8,128)(2,1)S(1)} %get-tuple-element.136, bf16[8,2,1,512,64]{3,4,1,2,0:T(8,128)(2,1)} %get-tuple-element.135, s32[]{:T(128)} %get-tuple-element.126), kind=kOutput, calls=%fused_computation.1.clone.1 | convolution fusion | flops 570110976 | bytes 18665680 | tf_op jit(solution)/shard_map/while/body/eval_jaxpr/ghqe,ghke->ghqk/dot_general | solution.py:112
  233.8 3.6 %fusion.94 = f32[8,2,1,512,64]{3,4,1,2,0:T(8,128)} fusion(f32[8,2,1,512,64]{3,4,1,2,0:T(8,128)} %get-tuple-element.127, s32[]{:T(128)} %get-tuple-element.126, bf16[2,1,4250,64]{2,3,0,1:T(8,128)(2,1)S(1)} %get-tuple-element.138, f32[2,512,4250]{1,2,0:T(8,128)S(1)} %get-tuple-element.117, f32[2,4250]{1,0:T(2,128)S(1)} %get-tuple-element.137, ...), kind=kOutput, calls=%fused_computation.9.clone.1 | convolution fusion | flops 570177536 | bytes 18796752 | tf_op jit(solution)/shard_map/while/body/eval_jaxpr/ghqk,ghke->ghqe/dot_general | solution.py:117
  237.5 4.8 %fusion.93 = (f32[2,512]{1,0:T(2,128)S(1)}, f32[2,512,4250]{1,2,0:T(8,128)S(1)}) fusion(f32[2,4250]{1,0:T(2,128)S(1)} %get-tuple-element.137, bf16[2,1,4250,64]{2,3,0,1:T(8,128)(2,1)S(1)} %get-tuple-element.136, bf16[8,2,1,512,64]{3,4,1,2,0:T(8,128)(2,1)} %get-tuple-element.135, s32[]{:T(128)} %get-tuple-element.126), kind=kOutput, calls=%fused_computation.1.clone.1 | convolution fusion | flops 570110976 | bytes 18665680 | tf_op jit(solution)/shard_map/while/body/eval_jaxpr/ghqe,ghke->ghqk/dot_general | solution.py:112
  242.2 3.6 %fusion.94 = f32[8,2,1,512,64]{3,4,1,2,0:T(8,128)} fusion(f32[8,2,1,512,64]{3,4,1,2,0:T(8,128)} %get-tuple-element.127, s32[]{:T(128)} %get-tuple-element.126, bf16[2,1,4250,64]{2,3,0,1:T(8,128)(2,1)S(1)} %get-tuple-element.138, f32[2,512,4250]{1,2,0:T(8,128)S(1)} %get-tuple-element.117, f32[2,4250]{1,0:T(2,128)S(1)} %get-tuple-element.137, ...), kind=kOutput, calls=%fused_computation.9.clone.1 | convolution fusion | flops 570177536 | bytes 18796752 | tf_op jit(solution)/shard_map/while/body/eval_jaxpr/ghqk,ghke->ghqe/dot_general | solution.py:117
  245.9 4.8 %fusion.93 = (f32[2,512]{1,0:T(2,128)S(1)}, f32[2,512,4250]{1,2,0:T(8,128)S(1)}) fusion(f32[2,4250]{1,0:T(2,128)S(1)} %get-tuple-element.137, bf16[2,1,4250,64]{2,3,0,1:T(8,128)(2,1)S(1)} %get-tuple-element.136, bf16[8,2,1,512,64]{3,4,1,2,0:T(8,128)(2,1)} %get-tuple-element.135, s32[]{:T(128)} %get-tuple-element.126), kind=kOutput, calls=%fused_computation.1.clone.1 | convolution fusion | flops 570110976 | bytes 18665680 | tf_op jit(solution)/shard_map/while/body/eval_jaxpr/ghqe,ghke->ghqk/dot_general | solution.py:112
  250.7 3.6 %fusion.94 = f32[8,2,1,512,64]{3,4,1,2,0:T(8,128)} fusion(f32[8,2,1,512,64]{3,4,1,2,0:T(8,128)} %get-tuple-element.127, s32[]{:T(128)} %get-tuple-element.126, bf16[2,1,4250,64]{2,3,0,1:T(8,128)(2,1)S(1)} %get-tuple-element.138, f32[2,512,4250]{1,2,0:T(8,128)S(1)} %get-tuple-element.117, f32[2,4250]{1,0:T(2,128)S(1)} %get-tuple-element.137, ...), kind=kOutput, calls=%fused_computation.9.clone.1 | convolution fusion | flops 570177536 | bytes 18796752 | tf_op jit(solution)/shard_map/while/body/eval_jaxpr/ghqk,ghke->ghqe/dot_general | solution.py:117
  254.3 4.8 %fusion.93 = (f32[2,512]{1,0:T(2,128)S(1)}, f32[2,512,4250]{1,2,0:T(8,128)S(1)}) fusion(f32[2,4250]{1,0:T(2,128)S(1)} %get-tuple-element.137, bf16[2,1,4250,64]{2,3,0,1:T(8,128)(2,1)S(1)} %get-tuple-element.136, bf16[8,2,1,512,64]{3,4,1,2,0:T(8,128)(2,1)} %get-tuple-element.135, s32[]{:T(128)} %get-tuple-element.126), kind=kOutput, calls=%fused_computation.1.clone.1 | convolution fusion | flops 570110976 | bytes 18665680 | tf_op jit(solution)/shard_map/while/body/eval_jaxpr/ghqe,ghke->ghqk/dot_general | solution.py:112
  259.1 3.6 %fusion.94 = f32[8,2,1,512,64]{3,4,1,2,0:T(8,128)} fusion(f32[8,2,1,512,64]{3,4,1,2,0:T(8,128)} %get-tuple-element.127, s32[]{:T(128)} %get-tuple-element.126, bf16[2,1,4250,64]{2,3,0,1:T(8,128)(2,1)S(1)} %get-tuple-element.138, f32[2,512,4250]{1,2,0:T(8,128)S(1)} %get-tuple-element.117, f32[2,4250]{1,0:T(2,128)S(1)} %get-tuple-element.137, ...), kind=kOutput, calls=%fused_computation.9.clone.1 | convolution fusion | flops 570177536 | bytes 18796752 | tf_op jit(solution)/shard_map/while/body/eval_jaxpr/ghqk,ghke->ghqe/dot_general | solution.py:117
  262.7 4.1 %copy.91 = f32[2,1,8,512,64]{3,2,4,0,1:T(8,128)} copy(f32[2,1,8,512,64]{3,4,0,1,2:T(8,128)} %bitcast.19) | data formatting | bytes 4194304 | tf_op jit(solution)/shard_map/transpose | solution.py:131
  266.9 2.7 reshape.275
  271.4 3.9 %copy.92 = bf16[2,4096,64]{2,0,1:T(2,128)(2,1)} copy(bf16[2,4096,64]{1,2,0:T(8,128)(2,1)S(1)} %multiply_convert_fusion) | data formatting | bytes 2097152 | tf_op jit(solution)/shard_map/convert_element_type | solution.py:138
  275.3 5.9 %reshape.282 = bf16[32,2,8192]{2,1,0:T(2,128)(2,1)} reshape(bf16[4096,2,64]{2,1,0:T(2,128)(2,1)} %bitcast.116) | data formatting | bytes 2097152
  281.1 5.0 %all-to-all-start.1 = ((bf16[32,2,8192]{2,1,0:T(2,128)(2,1)}), bf16[32,2,8192]{2,1,0:T(2,128)(2,1)S(1)}, u32[]{:S(2)}, u32[]{:S(2)}) async-start(bf16[32,2,8192]{2,1,0:T(2,128)(2,1)} %reshape.282), calls=%async_computation.1 | async-start | bytes 2097152 | tf_op jit(solution)/shard_map/all_to_all | solution.py:140
  289.5 13.6 %all-to-all-done.1 = bf16[32,2,8192]{2,1,0:T(2,128)(2,1)S(1)} async-done(((bf16[32,2,8192]{2,1,0:T(2,128)(2,1)}), bf16[32,2,8192]{2,1,0:T(2,128)(2,1)S(1)}, u32[]{:S(2)}, u32[]{:S(2)}) %all-to-all-start.1) | async-done | bytes 1048608 | tf_op jit(solution)/shard_map/all_to_all | solution.py:140
  305.4 5.0 %copy.99 = bf16[2,32,128,64]{2,3,1,0:T(8,128)(2,1)S(1)} copy(bf16[2,32,128,64]{3,0,2,1:T(2,128)(2,1)} %bitcast.117) | data formatting | bytes 2097152 | tf_op jit(solution)/shard_map/all_to_all | solution.py:140
  (72 shorter events, 28.9 us)
Async XLA Ops:
  7.2 1.6 copy-start
  7.2 30.6 %copy-start.8 = (s32[2]{0:T(128)S(1)}, s32[2]{0:T(128)}, u32[]{:S(2)}) copy-start(s32[2]{0:T(128)} %param.19) | copy-start | bytes 28
  7.2 108.1 %all-gather.3.cloned.1.call-start = ((), (), s32[]{:S(2)}) async-start(), calls=%async_computation.2 | async-start | bytes 30117888 | tf_op jit(solution)/shard_map/all_gather | solution.py:83
  10.7 30.7 %copy-start.2 = (bf16[2,154,2432]{2,0,1:T(2,128)(2,1)S(1)}, bf16[2,154,2432]{2,0,1:T(2,128)(2,1)}, u32[]{:S(2)}) copy-start(bf16[2,154,2432]{2,0,1:T(2,128)(2,1)} %param.16) | copy-start | bytes 4494340
  37.6 77.7 %copy-start.3 = (bf16[2,128,2432]{2,1,0:T(8,128)(2,1)S(1)}, bf16[2,128,2432]{2,1,0:T(8,128)(2,1)}, u32[]{:S(2)}) copy-start(bf16[2,128,2432]{2,1,0:T(8,128)(2,1)} %param.15) | copy-start | bytes 3735556
  128.9 1.0 copy-start.10
  128.9 1.0 copy-start.11
  133.1 46.1 %all-to-all-start = ((bf16[2,128,32,192]{1,3,0,2:T(8,128)(2,1)}), bf16[2,128,32,192]{1,3,0,2:T(8,128)(2,1)}, u32[]{:S(2)}, u32[]{:S(2)}) async-start(bf16[2,128,32,192]{1,3,0,2:T(8,128)(2,1)} %copy.78), calls=%async_computation | async-start | bytes 6291456 | tf_op jit(solution)/shard_map/all_to_all | solution.py:87
  139.4 5.1 %copy-start.12 = (bf16[2432,192]{0,1:T(8,128)(2,1)S(1)}, bf16[2432,192]{0,1:T(8,128)(2,1)}, u32[]{:S(2)}) copy-start(bf16[2432,192]{0,1:T(8,128)(2,1)} %param.23) | copy-start | bytes 2801668
  144.5 0.8 copy-start.9
  192.8 2.1 copy-start.6
  192.8 2.1 copy-start.4
  275.3 10.9 %copy-start.7 = (bf16[2,1,4096,64]{2,3,0,1:T(8,128)(2,1)S(1)}, bf16[2,1,4096,64]{2,3,0,1:T(8,128)(2,1)}, u32[]{:S(2)}) copy-start(bf16[2,1,4096,64]{2,3,0,1:T(8,128)(2,1)} %copy-done.6) | copy-start | bytes 3145732
  275.3 10.9 %copy-start.13 = (f32[64]{0:T(128)S(1)}, f32[64]{0:T(128)}, u32[]{:S(2)}) copy-start(f32[64]{0:T(128)} %param.26) | copy-start | bytes 772
  281.1 21.9 %all-to-all-start.1 = ((bf16[32,2,8192]{2,1,0:T(2,128)(2,1)}), bf16[32,2,8192]{2,1,0:T(2,128)(2,1)S(1)}, u32[]{:S(2)}, u32[]{:S(2)}) async-start(bf16[32,2,8192]{2,1,0:T(2,128)(2,1)} %reshape.282), calls=%async_computation.1 | async-start | bytes 2097152 | tf_op jit(solution)/shard_map/all_to_all | solution.py:140
  286.2 1.6 copy-start.5
  305.4 6.3 %copy-start.1 = (bf16[2432,304]{0,1:T(8,128)(2,1)S(1)}, bf16[2432,304]{0,1:T(8,128)(2,1)}, u32[]{:S(2)}) copy-start(bf16[2432,304]{0,1:T(8,128)(2,1)} %param.21) | copy-start | bytes 4435972
Sparse Core Ops, SparseCore 0:
  11.0 104.2 all-gather.2
where the time goes:
time: 320 us; the launch traced here: 319 us
  waiting for transfers between devices  121 us (38%)
  matrix products  86.9 us (27%)
  local copies, waits for them, and re-layouts  43 us (13%)
  blocking collectives  26.9 us (8%)
  other arithmetic  15.2 us (5%)
  between operations  14.4 us (4%)
  starting transfers between devices  11.3 us (4%)
    all_gather x1, waiting for transfers between devices, local(): lax.all_gather(w_img, ('req', 'tile'), axis=1, tiled=True)  72.7 us
    dot_general x9, matrix products, attend_block(): jnp.einsum('ghqe,ghke->ghqk', query_block, keys, preferred_element_type=j...  39.9 us
    all_to_all x1, waiting for transfers between devices, local(): lax.all_to_all(packed, 'tile', split_axis=2, concat_axis=1, tiled=True)  33.8 us
    dot_general x9, matrix products, attend_block(): jnp.einsum('ghqk,ghke->ghqe', weights.astype(jnp.bfloat16), values, prefe...  30.8 us
    all_gather x1, blocking collectives, local(): modulation = lax.all_gather(mod_part, 'tile', axis=1, tiled=True)  26.9 us
    dot_general x1, matrix products, local(): jnp.einsum('gpd,dc->gpc', h_img, lax.all_gather(w_img, ('req', 'tile'), a...  13.6 us
    all_to_all x1, waiting for transfers between devices, local(): lax.all_to_all(image_heads, 'tile', split_axis=1, concat_axis=2, tiled=True)  13.6 us
    unnamed x33, local copies, waits for them, and re-layouts  10.1 us
  transfers between devices with their start and end apart: 3, of which 3 were waited for; matrix products, arithmetic and copies ran while one was open for 5% of the time, Pallas kernels for 0%

commit v1 on v0

--- a/solution.py
+++ b/solution.py
@@ -80,7 +80,12 @@
     qkv_img = jnp.einsum(
         "gpd,dc->gpc",
         h_img,
-        lax.all_gather(w_img, ("req", "tile"), axis=1, tiled=True),
+        jnp.concatenate(
+            lax.all_to_all(
+                jnp.stack([w_img] * lax.axis_size(("req", "tile"))), ("req", "tile"), 0, 0
+            ),
+            axis=1,
+        ),
         preferred_element_type=jnp.float32,
     )
     packed = pack_heads(qkv_img, head_dim, q_gain, k_gain)

time: 320 us -> 694 us (2.17)
  blocking collectives: 26.9 us -> 463 us
  waiting for transfers between devices: 121 us -> 47.3 us
  between operations: 14.4 us -> 1.07 us
  local copies, waits for them, and re-layouts: 43 us -> 53.9 us
  starting transfers between devices: 11.3 us -> 21.6 us
    all_gather x1, blocking collectives: 26.9 us -> 463 us  [local(): modulation = lax.all_gather(mod_part, 'tile', axis=1, tiled=True)]
    all_gather x1 -> x0, waiting for transfers between devices: 72.7 us -> none  [local(): lax.all_gather(w_img, ('req', 'tile'), axis=1, tiled=True)]
    all_to_all x0 -> x1, starting transfers between devices: none -> 11.9 us  [local(): lax.all_to_all(jnp.stack([w_img] * lax.axis_size(('req', 'tile'))), ('req...]
    another operation x0 -> x1, local copies, waits for them, and re-layouts: none -> 10.9 us  [local(): jnp.stack([w_img] * lax.axis_size(('req', 'tile')))]
  transfers between devices with their start and end apart: 3 -> 3, of which waited for: 3 -> 2; matrix products, arithmetic and copies ran while one was open for 5% -> 2% of each run, Pallas kernels for 0% -> 0%
where the time goes in v1:
time: 694 us; the launch traced here: 690 us
  blocking collectives  463 us (67%)
  matrix products  89.6 us (13%)
  local copies, waits for them, and re-layouts  53.9 us (8%)
  waiting for transfers between devices  47.3 us (7%)
  starting transfers between devices  21.6 us (3%)
  other arithmetic  13.2 us (2%)
    all_gather x1, blocking collectives, local(): modulation = lax.all_gather(mod_part, 'tile', axis=1, tiled=True)  463 us
    dot_general x9, matrix products, attend_block(): jnp.einsum('ghqe,ghke->ghqk', query_block, keys, preferred_element_type=j...  40 us
    all_to_all x1, waiting for transfers between devices, local(): lax.all_to_all(packed, 'tile', split_axis=2, concat_axis=1, tiled=True)  33.7 us
    dot_general x9, matrix products, attend_block(): jnp.einsum('ghqk,ghke->ghqe', weights.astype(jnp.bfloat16), values, prefe...  30.7 us
    dot_general x1, matrix products, local(): jnp.einsum('gpd,dc->gpc', h_img, jnp.concatenate(lax.all_to_all(jnp.stack...  16.2 us
  transfers between devices with their start and end apart: 3, of which 2 were waited for; matrix products, arithmetic and copies ran while one was open for 2% of the time, Pallas kernels for 0%

profile of v1, /device:TPU:1, one launch (start us, length us, event | category | flops | bytes accessed | tf_op | source)
XLA Modules:
  0.0 690.0 jit_solution(4450447239714247921)
XLA Ops:
  0.6 10.9 %stack.2 = bf16[128,2432,48]{1,2,0:T(8,128)(2,1)} broadcast(bf16[2432,48]{0,1:T(8,128)(2,1)} %param.22), dimensions={1,2} | broadcast | bytes 30117888 | tf_op jit(solution)/shard_map/stack | solution.py:85
  11.5 11.9 %all-to-all-start = ((bf16[128,2432,48]{1,2,0:T(8,128)(2,1)}), bf16[128,2432,48]{1,2,0:T(8,128)(2,1)}, u32[]{:S(2)}, u32[]{:S(2)}) async-start(bf16[128,2432,48]{1,2,0:T(8,128)(2,1)} %stack.2), calls=%async_computation | async-start | bytes 59768832 | tf_op jit(solution)/shard_map/all_to_all | solution.py:84
  25.7 463.3 %all-gather = bf16[32,304,2]{1,2,0:T(2,128)(2,1)S(1)} all-gather(bf16[1,304,2]{1,2,0:T(2,128)(2,1)S(1)} %fusion.59), channel_id=1, replica_groups=mesh['req'=4,'tile'=32] {'tile'}, dimensions={0}, use_global_device_ids=true | all-gather | bytes 40128 | tf_op jit(solution)/shard_map/all_gather | solution.py:74
  492.7 16.2 %fusion.45 = f32[2,128,32,3,64]{1,4,3,2,0:T(8,128)S(1)} fusion(bf16[32,3,64,2432,1]{3,2,1,0,4:T(8,128)(2,1)} %bitcast.13, bf16[2,128,2432]{2,1,0:T(8,128)(2,1)S(1)} %copy-done.3, f32[2,2432]{1,0:T(2,128)S(1)} %get-tuple-element.69, f32[2,2432]{1,0:T(2,128)S(1)} %get-tuple-element.67, f32[2,128]{1,0:T(2,128)S(1)} %add_rsqrt_fusion.5, ...), kind=kOutput, calls=%fused_computation.46 | convolution fusion | flops 7654146048 | bytes 37462016 | tf_op jit(solution)/shard_map/gpd,dc->gpc/dot_general | solution.py:80
  513.1 4.8 all-to-all-start.1
  520.1 3.0 fusion.33
  523.9 33.7 %all-to-all-done.1 = bf16[2,128,32,192]{1,3,0,2:T(8,128)(2,1)} async-done(((bf16[2,128,32,192]{1,3,0,2:T(8,128)(2,1)}), bf16[2,128,32,192]{1,3,0,2:T(8,128)(2,1)}, u32[]{:S(2)}, u32[]{:S(2)}) %all-to-all-start.1) | async-done | bytes 3145760 | tf_op jit(solution)/shard_map/all_to_all | solution.py:92
  557.6 5.6 copy.75
  563.2 5.8 reshape.281
  573.7 67.4 %while.10 = (s32[]{:T(128)}, f32[8,2,1,512,64]{3,4,1,2,0:T(8,128)}, bf16[8,2,1,512,64]{3,4,1,2,0:T(8,128)(2,1)}, bf16[2,1,4250,64]{2,3,0,1:T(8,128)(2,1)S(1)}, f...) while((s32[]{:T(128)}, f32[8,2,1,512,64]{3,4,1,2,0:T(8,128)}, ...), condition=%wide.region_9.10_spmd, body=%wide.region_7.0_spmd.sunk | while | flops 1140288512 | bytes 37462508 | solution.py:135
  573.7 4.8 fusion.94
  578.6 3.6 fusion.95
  582.2 4.8 fusion.94
  587.0 3.6 fusion.95
  590.6 4.8 fusion.94
  595.4 3.6 fusion.95
  599.0 4.8 fusion.94
  603.8 3.6 fusion.95
  607.4 4.8 fusion.94
  612.2 3.6 fusion.95
  615.9 4.8 fusion.94
  620.7 3.6 fusion.95
  624.3 4.8 fusion.94
  629.1 3.6 fusion.95
  632.7 4.8 fusion.94
  637.5 3.6 fusion.95
  641.1 4.1 copy.87
  649.8 3.9 copy.88
  653.7 5.9 reshape.291
  659.5 4.9 all-to-all-start.2
  667.8 13.6 %all-to-all-done.2 = bf16[32,2,8192]{2,1,0:T(2,128)(2,1)S(1)} async-done(((bf16[32,2,8192]{2,1,0:T(2,128)(2,1)}), bf16[32,2,8192]{2,1,0:T(2,128)(2,1)S(1)}, u32[]{:S(2)}, u32[]{:S(2)}) %all-to-all-start.2) | async-done | bytes 1048608 | tf_op jit(solution)/shard_map/all_to_all | solution.py:145
  683.7 5.0 copy.95
  (76 shorter events, 29.0 us)
Async XLA Ops:
  0.6 23.0 %copy-start = (bf16[2432,304]{0,1:T(8,128)(2,1)S(1)}, bf16[2432,304]{0,1:T(8,128)(2,1)}, u32[]{:S(2)}) copy-start(bf16[2432,304]{0,1:T(8,128)(2,1)} %param.21) | copy-start | bytes 4435972
  11.5 11.9 %copy-start.14 = (s32[2]{0:T(128)S(1)}, s32[2]{0:T(128)}, u32[]{:S(2)}) copy-start(s32[2]{0:T(128)} %param.18) | copy-start | bytes 28
  11.5 12.1 %copy-start.8 = (f32[2,2432]{1,0:T(2,128)S(1)}, f32[2,2432]{1,0:T(2,128)}, u32[]{:S(2)}) copy-start(f32[2,2432]{1,0:T(2,128)} %param.17) | copy-start | bytes 58372
  11.5 481.2 %all-to-all-start = ((bf16[128,2432,48]{1,2,0:T(8,128)(2,1)}), bf16[128,2432,48]{1,2,0:T(8,128)(2,1)}, u32[]{:S(2)}, u32[]{:S(2)}) async-start(bf16[128,2432,48]{1,2,0:T(8,128)(2,1)} %stack.2), calls=%async_computation | async-start | bytes 59768832 | tf_op jit(solution)/shard_map/all_to_all | solution.py:84
  23.4 465.7 %copy-start.9 = (s32[2]{0:T(128)S(1)}, s32[2]{0:T(128)}, u32[]{:S(2)}) copy-start(s32[2]{0:T(128)} %param.19) | copy-start | bytes 28
  23.6 467.8 %copy-start.2 = (bf16[2,154,2432]{2,0,1:T(2,128)(2,1)S(1)}, bf16[2,154,2432]{2,0,1:T(2,128)(2,1)}, u32[]{:S(2)}) copy-start(bf16[2,154,2432]{2,0,1:T(2,128)(2,1)} %param.16) | copy-start | bytes 4494340
  25.7 465.2 %copy-start.3 = (bf16[2,128,2432]{2,1,0:T(8,128)(2,1)S(1)}, bf16[2,128,2432]{2,1,0:T(8,128)(2,1)}, u32[]{:S(2)}) copy-start(bf16[2,128,2432]{2,1,0:T(8,128)(2,1)} %param.15) | copy-start | bytes 3735556
  508.9 1.0 copy-start.11
  508.9 1.0 copy-start.12
  513.1 44.5 %all-to-all-start.1 = ((bf16[2,128,32,192]{1,3,0,2:T(8,128)(2,1)}), bf16[2,128,32,192]{1,3,0,2:T(8,128)(2,1)}, u32[]{:S(2)}, u32[]{:S(2)}) async-start(bf16[2,128,32,192]{1,3,0,2:T(8,128)(2,1)} %copy.74), calls=%async_computation.1 | async-start | bytes 6291456 | tf_op jit(solution)/shard_map/all_to_all | solution.py:92
  517.9 5.1 copy-start.13
  523.1 0.8 copy-start.10
  571.2 2.1 copy-start.6
  571.2 2.1 copy-start.4
  653.7 10.8 %copy-start.7 = (bf16[2,1,4096,64]{2,3,0,1:T(8,128)(2,1)S(1)}, bf16[2,1,4096,64]{2,3,0,1:T(8,128)(2,1)}, u32[]{:S(2)}) copy-start(bf16[2,1,4096,64]{2,3,0,1:T(8,128)(2,1)} %copy-done.6) | copy-start | bytes 3145732
  653.7 10.8 %copy-start.15 = (f32[64]{0:T(128)S(1)}, f32[64]{0:T(128)}, u32[]{:S(2)}) copy-start(f32[64]{0:T(128)} %param.26) | copy-start | bytes 772
  659.5 21.8 %all-to-all-start.2 = ((bf16[32,2,8192]{2,1,0:T(2,128)(2,1)}), bf16[32,2,8192]{2,1,0:T(2,128)(2,1)S(1)}, u32[]{:S(2)}, u32[]{:S(2)}) async-start(bf16[32,2,8192]{2,1,0:T(2,128)(2,1)} %reshape.291), calls=%async_computation.2 | async-start | bytes 2097152 | tf_op jit(solution)/shard_map/all_to_all | solution.py:145
  664.5 1.6 copy-start.5
  683.7 6.3 copy-start.1
